TPU v7x, 32 devices: a whole 2x2x4 slice. The times are simulated.
32 devices in a mesh: groups: 2 (over y), chan: 4 (over z), space: 4 (over x, core).
Axes of the slice: x: 2, y: 2, z: 4, core: 2. Of those that a mesh axis runs over, the one named last changes fastest.
Arguments:
- volume: bfloat16 [2048, 16, 512], P(('groups', 'chan'), 'space'), parts along dimension 0, may hold values from -6 to 6
- out_grad: bfloat16 [2048, 16, 512], P(('groups', 'chan'), 'space'), parts along dimension 0, may hold values from -6 to 6
- weight_in: bfloat16 [1024, 1024], P('chan'), may hold values from -0.1875 to 0.1875
- weight_out: bfloat16 [1024, 1024], P('chan'), may hold values from -0.1875 to 0.1875
- filter_taps: float32 [1024, 27], P('chan'), may hold values from -1.25 to 1.25
- filter_bias: float32 [1024], P('chan'), may hold values from -3 to 3
Outputs:
- block_out: bfloat16 [2048, 16, 512], P(('groups', 'chan'), 'space'), parts along dimension 0
- volume_grad: bfloat16 [2048, 16, 512], P(('groups', 'chan'), 'space'), parts along dimension 0
There are 2 independent parts, one for each index of `groups`. A program takes and returns all parts, laid end to end along the dimension named above; an argument that names none is the same for every part. Nothing has to cross between parts.
All inputs are finite; a program needn't handle non-finite values.
Results may differ from a plain program's by a relative error of at most 0.0085.
Values may be sent and summed in bfloat16 or wider, within the bound.
No kernel may reach another device: no remote copies, remote signals or barrier semaphores. Data moves between devices by JAX's collectives and lax.ppermute only.
A program may use at most 64 MiB of HBM per device.

v0:
```python
import jax
import jax.numpy as jnp
from jax import lax
from jax.sharding import PartitionSpec as P

CX = 32
CY = 16
root_half = 0.7071067811865476
inv_root_two_pi = 0.3989422804014327


def with_halo(block, sides, width):
    for axis, dim in sides:
        count = lax.axis_size(axis)
        forward = [(i, i + 1) for i in range(count - 1)]
        backward = [(target, source) for source, target in forward]
        low = lax.ppermute(
            lax.slice_in_dim(block, block.shape[dim] - width, None, axis=dim), axis, forward
        )
        high = lax.ppermute(lax.slice_in_dim(block, 0, width, axis=dim), axis, backward)
        block = jnp.concatenate([low, block, high], axis=dim)
    return block


def gelu_value(field):
    return 0.5 * field * (1.0 + lax.erf(field * root_half))


def gelu_slope(field):
    return (
        0.5 * (1.0 + lax.erf(field * root_half))
        + field * jnp.exp(-0.5 * field * field) * inv_root_two_pi
    )


def core(padded, filter_taps, direction):
    extent_z = padded.shape[1] - 2
    extent_y = padded.shape[2] - 2
    extent_x = padded.shape[3] - 2
    summed = jnp.zeros((padded.shape[0], extent_z, extent_y, extent_x), jnp.float32)
    for shift_z in range(3):
        for shift_y in range(3):
            for shift_x in range(3):
                tap_index = (shift_z * 3 + shift_y) * 3 + shift_x
                begin_z = 1 + direction * (shift_z - 1)
                begin_y = 1 + direction * (shift_y - 1)
                begin_x = 1 + direction * (shift_x - 1)
                window = padded[
                    :,
                    begin_z : begin_z + extent_z,
                    begin_y : begin_y + extent_y,
                    begin_x : begin_x + extent_x,
                ]
                summed = summed + filter_taps[:, tap_index][:, None, None, None] * window
    return summed


def lift(field_z):
    extended = field_z.astype(jnp.float32).reshape(field_z.shape[0], field_z.shape[1], CY, CX)
    return jnp.pad(extended, ((0, 0), (0, 0), (1, 1), (1, 1)))


def to_cells(field):
    return lax.all_to_all(
        field.reshape(field.shape[0], -1), "chan", split_axis=1, concat_axis=0, tiled=True
    )


def to_channels(field, slab_shape):
    return lax.all_to_all(field, "chan", split_axis=0, concat_axis=1, tiled=True).reshape(
        slab_shape
    )


def body(volume, out_grad, weight_in, weight_out, filter_taps, filter_bias):
    slab_shape = volume.shape
    contract_first = (((0,), (0,)), ((), ()))
    full_in, full_out = (
        lax.all_gather(weight_in, "chan", axis=0, tiled=True),
        lax.all_gather(weight_out, "chan", axis=0, tiled=True),
    )
    vol_cells = to_cells(volume)
    hidden = to_channels(
        jnp.dot(full_in, vol_cells, preferred_element_type=jnp.float32).astype(jnp.bfloat16),
        slab_shape,
    )
    padded = lift(with_halo(hidden, (("space", 1),), 1))
    mixed = core(padded, filter_taps, 1) + filter_bias[:, None, None, None]
    active = gelu_value(mixed).astype(jnp.bfloat16).reshape(slab_shape)
    act_cells = to_cells(active)
    out_cells = vol_cells.astype(jnp.float32) + jnp.dot(
        full_out, act_cells, preferred_element_type=jnp.float32
    )
    block_out = to_channels(out_cells.astype(jnp.bfloat16), slab_shape)
    grad_cells = to_cells(out_grad)
    act_part = lax.dot_general(
        full_out, grad_cells, contract_first, preferred_element_type=jnp.float32
    )
    act_grad = to_channels(act_part.astype(jnp.bfloat16), slab_shape)
    slope = gelu_slope(mixed)
    mix_grad = (
        (act_grad.astype(jnp.float32).reshape(slope.shape) * slope)
        .astype(jnp.bfloat16)
        .reshape(slab_shape)
    )
    padded_grad = lift(with_halo(mix_grad, (("space", 1),), 1))
    hid_grad = core(padded_grad, filter_taps, -1).astype(jnp.bfloat16).reshape(slab_shape)
    hid_cells = to_cells(hid_grad)
    back_part = lax.dot_general(
        full_in, hid_cells, contract_first, preferred_element_type=jnp.float32
    )
    volume_grad = to_channels(
        (grad_cells.astype(jnp.float32) + back_part).astype(jnp.bfloat16), slab_shape
    )
    return (block_out, volume_grad)


def solution(mesh):
    placed = (
        P(("groups", "chan"), "space", None),
        P(("groups", "chan"), "space", None),
        P("chan", None),
        P("chan", None),
        P("chan", None),
        P("chan"),
    )
    return jax.shard_map(
        body,
        mesh=mesh,
        in_specs=placed,
        out_specs=(P(("groups", "chan"), "space", None), P(("groups", "chan"), "space", None)),
        check_vma=False,
    )
```

profile of v0, /device:TPU:0, one launch (start us, length us, event | category | flops | bytes accessed | tf_op | source)
XLA Modules:
  0.0 338.6 jit_solution(1226160043802990815)
XLA Ops:
  7.9 2.5 copy.26
  10.4 6.3 %all-to-all-start = ((bf16[256,4,512]{2,0,1:T(8,128)(2,1)}), bf16[256,4,512]{2,0,1:T(8,128)(2,1)S(1)}, u32[]{:S(2)}, u32[]{:S(2)}) async-start(bf16[256,4,512]{2,0,1:T(8,128)(2,1)} %copy.26), calls=%async_computation | async-start | bytes 2097152 | tf_op jit(solution)/shard_map/all_to_all | solution.py:64
  18.6 49.2 %all-to-all-done = bf16[256,4,512]{2,0,1:T(8,128)(2,1)S(1)} async-done(((bf16[256,4,512]{2,0,1:T(8,128)(2,1)}), bf16[256,4,512]{2,0,1:T(8,128)(2,1)S(1)}, u32[]{:S(2)}, u32[]{:S(2)}) %all-to-all-start) | async-done | bytes 1048608 | tf_op jit(solution)/shard_map/all_to_all | solution.py:64
  67.8 3.5 %all-to-all-start.4 = ((bf16[256,4,512]{2,0,1:T(8,128)(2,1)}), bf16[256,4,512]{2,0,1:T(8,128)(2,1)S(1)}, u32[]{:S(2)}, u32[]{:S(2)}) async-start(bf16[256,4,512]{2,0,1:T(8,128)(2,1)} %copy.31), calls=%async_computation.4 | async-start | bytes 2097152 | tf_op jit(solution)/shard_map/all_to_all | solution.py:64
  71.3 15.1 %all-gather.3.cloned.1.call-done = bf16[1024,1024]{1,0:T(8,128)(2,1)} async-done(((bf16[256,1024]{1,0:T(8,128)(2,1)}), bf16[1024,1024]{1,0:T(8,128)(2,1)}) %all-gather.3.cloned.1.call-update) | async-done | bytes 2097168 | tf_op jit(solution)/shard_map/all_gather | solution.py:79
  86.5 2.8 convolution_convert_fusion.1
  90.7 8.0 %all-to-all-done.4 = bf16[256,4,512]{2,0,1:T(8,128)(2,1)S(1)} async-done(((bf16[256,4,512]{2,0,1:T(8,128)(2,1)}), bf16[256,4,512]{2,0,1:T(8,128)(2,1)S(1)}, u32[]{:S(2)}, u32[]{:S(2)}) %all-to-all-start.4) | async-done | bytes 1048608 | tf_op jit(solution)/shard_map/all_to_all | solution.py:64
  98.7 3.5 %all-to-all-start.1 = ((bf16[4,256,512]{1,2,0:T(8,128)(2,1)}), bf16[4,256,512]{1,2,0:T(8,128)(2,1)S(1)}, u32[]{:S(2)}, u32[]{:S(2)}) async-start(bf16[4,256,512]{1,2,0:T(8,128)(2,1)} %copy.28), calls=%async_computation.1 | async-start | bytes 2097152 | tf_op jit(solution)/shard_map/all_to_all | solution.py:70
  102.3 58.4 %all-gather.5.cloned.1.call-done = bf16[1024,1024]{1,0:T(8,128)(2,1)} async-done(((bf16[256,1024]{1,0:T(8,128)(2,1)}), bf16[1024,1024]{1,0:T(8,128)(2,1)}) %all-gather.5.cloned.1.call-update) | async-done | bytes 2097168 | tf_op jit(solution)/shard_map/all_gather | solution.py:80
  160.6 2.9 convolution_convert_fusion
  164.8 3.6 %all-to-all-start.5 = ((bf16[4,256,512]{1,2,0:T(8,128)(2,1)}), bf16[4,256,512]{1,2,0:T(8,128)(2,1)S(1)}, u32[]{:S(2)}, u32[]{:S(2)}) async-start(bf16[4,256,512]{1,2,0:T(8,128)(2,1)} %copy.33), calls=%async_computation.5 | async-start | bytes 2097152 | tf_op jit(solution)/shard_map/all_to_all | solution.py:70
  172.3 22.0 %all-to-all-done.5 = bf16[4,256,512]{1,2,0:T(8,128)(2,1)S(1)} async-done(((bf16[4,256,512]{1,2,0:T(8,128)(2,1)}), bf16[4,256,512]{1,2,0:T(8,128)(2,1)S(1)}, u32[]{:S(2)}, u32[]{:S(2)}) %all-to-all-start.5) | async-done | bytes 1048608 | tf_op jit(solution)/shard_map/all_to_all | solution.py:70
  195.7 10.0 %fusion.5 = (bf16[256,4,16,32]{0,3,2,1:T(8,128)(2,1)S(1)}, f32[256,4,16,32]{0,3,2,1:T(8,128)S(1)}) fusion(f32[256,4,16,32]{0,3,2,1:T(8,128)S(1)} %bitcast.72, f32[256]{0:T(256)S(1)} %copy-done.5, f32[256]{0:T(256)S(1)} %bitcast.102, f32[256]{0:T(256)S(1)} %bitcast.104, f32[256]{0:T(256)S(1)} %bitcast.108, f32[256]{0:T(256)S(1)} %bitcast.110, ...), kind=kLoop, calls=%fused_computation.54 | loop fusion | flops 33554432 | bytes 14708736 | tf_op jit(solution)/shard_map/convert_element_type | solution.py:103
  210.6 3.5 %all-to-all-start.2 = ((bf16[256,4,512]{0,2,1:T(8,128)(2,1)}), bf16[256,4,512]{0,2,1:T(8,128)(2,1)S(1)}, u32[]{:S(2)}, u32[]{:S(2)}) async-start(bf16[256,4,512]{0,2,1:T(8,128)(2,1)} %bitcast.35), calls=%async_computation.2 | async-start | bytes 2097152 | tf_op jit(solution)/shard_map/all_to_all | solution.py:64
  215.3 10.0 %fusion.104 = bf16[256,4,16,32]{0,3,2,1:T(8,128)(2,1)} fusion(f32[256,6,16,32]{0,3,2,1:T(8,128)S(1)} %maximum_convert_fusion.1, f32[256]{0:T(256)S(1)} %bitcast.103, f32[256]{0:T(256)S(1)} %bitcast.105, f32[256]{0:T(256)S(1)} %bitcast.109, f32[256]{0:T(256)S(1)} %bitcast.111, f32[256]{0:T(256)S(1)} %bitcast.113, f32[256]{0:T(256)S(1)} %bitcast.115, ...), kind=kLoop, calls=%fused_computation.153 | loop fusion | flops 28311552 | bytes 10513408 | tf_op jit(solution)/shard_map/convert_element_type | solution.py:107
  225.4 14.8 %all-to-all-done.2 = bf16[256,4,512]{0,2,1:T(8,128)(2,1)S(1)} async-done(((bf16[256,4,512]{0,2,1:T(8,128)(2,1)}), bf16[256,4,512]{0,2,1:T(8,128)(2,1)S(1)}, u32[]{:S(2)}, u32[]{:S(2)}) %all-to-all-start.2) | async-done | bytes 1048608 | tf_op jit(solution)/shard_map/all_to_all | solution.py:64
  240.2 4.3 %all-to-all-start.6 = ((bf16[256,4,512]{0,2,1:T(8,128)(2,1)}), bf16[256,4,512]{0,2,1:T(8,128)(2,1)}, u32[]{:S(2)}, u32[]{:S(2)}) async-start(bf16[256,4,512]{0,2,1:T(8,128)(2,1)} %bitcast.83), calls=%async_computation.6 | async-start | bytes 2097152 | tf_op jit(solution)/shard_map/all_to_all | solution.py:64
  247.1 3.2 fusion.109
  251.7 19.9 %all-to-all-done.6 = bf16[256,4,512]{0,2,1:T(8,128)(2,1)} async-done(((bf16[256,4,512]{0,2,1:T(8,128)(2,1)}), bf16[256,4,512]{0,2,1:T(8,128)(2,1)}, u32[]{:S(2)}, u32[]{:S(2)}) %all-to-all-start.6) | async-done | bytes 1048608 | tf_op jit(solution)/shard_map/all_to_all | solution.py:64
  271.5 3.7 %all-to-all-start.3 = ((bf16[4,256,512]{2,1,0:T(8,128)(2,1)}), bf16[4,256,512]{2,1,0:T(8,128)(2,1)S(1)}, u32[]{:S(2)}, u32[]{:S(2)}) async-start(bf16[4,256,512]{2,1,0:T(8,128)(2,1)} %bitcast.39), calls=%async_computation.3 | async-start | bytes 2097152 | tf_op jit(solution)/shard_map/all_to_all | solution.py:70
  277.3 3.8 %fusion.108 = bf16[1024,512]{0,1:T(8,128)(2,1)} fusion(bf16[1024,512]{0,1:T(8,128)(2,1)S(1)} %copy.40, bf16[1024,512]{1,0:T(8,128)(2,1)S(1)} %bitcast.85, bf16[1024,1024]{1,0:T(8,128)(2,1)} %all-gather.3.cloned.1.call-done), kind=kOutput, calls=%fused_computation.164 | convolution fusion | flops 1075314688 | bytes 5242880 | tf_op jit(solution)/shard_map/dot_general | solution.py:109
  283.4 17.8 %all-to-all-done.3 = bf16[4,256,512]{2,1,0:T(8,128)(2,1)S(1)} async-done(((bf16[4,256,512]{2,1,0:T(8,128)(2,1)}), bf16[4,256,512]{2,1,0:T(8,128)(2,1)S(1)}, u32[]{:S(2)}, u32[]{:S(2)}) %all-to-all-start.3) | async-done | bytes 1048608 | tf_op jit(solution)/shard_map/all_to_all | solution.py:70
  301.2 3.5 %all-to-all-start.7 = ((bf16[4,256,512]{2,1,0:T(8,128)(2,1)}), bf16[4,256,512]{2,1,0:T(8,128)(2,1)S(1)}, u32[]{:S(2)}, u32[]{:S(2)}) async-start(bf16[4,256,512]{2,1,0:T(8,128)(2,1)} %bitcast.54), calls=%async_computation.7 | async-start | bytes 2097152 | tf_op jit(solution)/shard_map/all_to_all | solution.py:70
  306.5 23.5 %all-to-all-done.7 = bf16[4,256,512]{2,1,0:T(8,128)(2,1)S(1)} async-done(((bf16[4,256,512]{2,1,0:T(8,128)(2,1)}), bf16[4,256,512]{2,1,0:T(8,128)(2,1)S(1)}, u32[]{:S(2)}, u32[]{:S(2)}) %all-to-all-start.7) | async-done | bytes 1048608 | tf_op jit(solution)/shard_map/all_to_all | solution.py:70
  (44 shorter events, 28.3 us)
Async XLA Ops:
  7.2 79.3 %all-gather.3.cloned.1.call-start = ((), (), s32[]{:S(2)}) async-start(), calls=%async_computation.8 | async-start | bytes 2621440 | tf_op jit(solution)/shard_map/all_gather | solution.py:79
  7.9 9.6 %copy-start.2 = (bf16[256,4,512]{2,1,0:T(4,128)(2,1)S(1)}, bf16[256,4,512]{2,1,0:T(4,128)(2,1)}, u32[]{:S(2)}) copy-start(bf16[256,4,512]{2,1,0:T(4,128)(2,1)} %param.7) | copy-start | bytes 3145732
  10.4 57.4 %all-to-all-start = ((bf16[256,4,512]{2,0,1:T(8,128)(2,1)}), bf16[256,4,512]{2,0,1:T(8,128)(2,1)S(1)}, u32[]{:S(2)}, u32[]{:S(2)}) async-start(bf16[256,4,512]{2,0,1:T(8,128)(2,1)} %copy.26), calls=%async_computation | async-start | bytes 2097152 | tf_op jit(solution)/shard_map/all_to_all | solution.py:64
  16.7 143.9 %all-gather.5.cloned.1.call-start = ((), (), s32[]{:S(2)}) async-start(), calls=%async_computation.9 | async-start | bytes 2621440 | tf_op jit(solution)/shard_map/all_gather | solution.py:80
  67.8 21.5 %copy-start = (bf16[256,4,512]{2,0,1:T(8,128)(2,1)}, bf16[256,4,512]{2,0,1:T(8,128)(2,1)S(1)}, u32[]{:S(2)}) copy-start(bf16[256,4,512]{2,0,1:T(8,128)(2,1)S(1)} %all-to-all-done) | copy-start | bytes 3145732
  67.8 30.9 %all-to-all-start.4 = ((bf16[256,4,512]{2,0,1:T(8,128)(2,1)}), bf16[256,4,512]{2,0,1:T(8,128)(2,1)S(1)}, u32[]{:S(2)}, u32[]{:S(2)}) async-start(bf16[256,4,512]{2,0,1:T(8,128)(2,1)} %copy.31), calls=%async_computation.4 | async-start | bytes 2097152 | tf_op jit(solution)/shard_map/all_to_all | solution.py:64
  98.7 66.1 %all-to-all-start.1 = ((bf16[4,256,512]{1,2,0:T(8,128)(2,1)}), bf16[4,256,512]{1,2,0:T(8,128)(2,1)S(1)}, u32[]{:S(2)}, u32[]{:S(2)}) async-start(bf16[4,256,512]{1,2,0:T(8,128)(2,1)} %copy.28), calls=%async_computation.1 | async-start | bytes 2097152 | tf_op jit(solution)/shard_map/all_to_all | solution.py:70
  164.8 7.4 %copy-start.4 = (f32[256,27]{0,1:T(8,128)S(1)}, f32[256,27]{0,1:T(8,128)}, u32[]{:S(2)}) copy-start(f32[256,27]{0,1:T(8,128)} %param.10) | copy-start | bytes 82948
  164.8 29.5 %all-to-all-start.5 = ((bf16[4,256,512]{1,2,0:T(8,128)(2,1)}), bf16[4,256,512]{1,2,0:T(8,128)(2,1)S(1)}, u32[]{:S(2)}, u32[]{:S(2)}) async-start(bf16[4,256,512]{1,2,0:T(8,128)(2,1)} %copy.33), calls=%async_computation.5 | async-start | bytes 2097152 | tf_op jit(solution)/shard_map/all_to_all | solution.py:70
  169.3 25.2 %collective-permute-start = (bf16[256,1,512]{0,2,1:T(8,128)(2,1)}, bf16[256,1,512]{0,2,1:T(8,128)(2,1)S(1)}, u32[]{:S(2)}, u32[]{:S(2)}) collective-permute-start(bf16[256,1,512]{0,2,1:T(8,128)(2,1)} %get-tuple-element.8), channel_id=1, source_target_pairs={{0,1},{1,2},{2,3},{4,5},{5,6},{6,7},{8,9},{9,10},{10,11},{12,13},{... | collective-permute-start | bytes 786440 | tf_op jit(solution)/shard_map/ppermute | solution.py:17
  170.9 23.6 %collective-permute-start.1 = (bf16[256,1,512]{0,2,1:T(8,128)(2,1)}, bf16[256,1,512]{0,2,1:T(8,128)(2,1)}, u32[]{:S(2)}, u32[]{:S(2)}) collective-permute-start(bf16[256,1,512]{0,2,1:T(8,128)(2,1)} %get-tuple-element.9), channel_id=1, source_target_pairs={{1,0},{2,1},{3,2},{5,4},{6,5},{7,6},{9,8},{10,9},{11,10},{13,12},{... | collective-permute-start | bytes 786440 | tf_op jit(solution)/shard_map/ppermute | solution.py:20
  194.5 1.2 copy-start.5
  206.6 7.5 %collective-permute-start.2 = (bf16[256,1,512]{0,2,1:T(8,128)(2,1)}, bf16[256,1,512]{0,2,1:T(8,128)(2,1)S(1)}, u32[]{:S(2)}, u32[]{:S(2)}) collective-permute-start(bf16[256,1,512]{0,2,1:T(8,128)(2,1)} %get-tuple-element.6), channel_id=1, source_target_pairs={{0,1},{1,2},{2,3},{4,5},{5,6},{6,7},{8,9},{9,10},{10,11},{12,13},{... | collective-permute-start | bytes 786440 | tf_op jit(solution)/shard_map/ppermute | solution.py:17
  207.9 6.2 %collective-permute-start.3 = (bf16[256,1,512]{0,2,1:T(8,128)(2,1)}, bf16[256,1,512]{0,2,1:T(8,128)(2,1)}, u32[]{:S(2)}, u32[]{:S(2)}) collective-permute-start(bf16[256,1,512]{0,2,1:T(8,128)(2,1)} %get-tuple-element.7), channel_id=1, source_target_pairs={{1,0},{2,1},{3,2},{5,4},{6,5},{7,6},{9,8},{10,9},{11,10},{13,12},{... | collective-permute-start | bytes 786440 | tf_op jit(solution)/shard_map/ppermute | solution.py:20
  210.6 29.6 %all-to-all-start.2 = ((bf16[256,4,512]{0,2,1:T(8,128)(2,1)}), bf16[256,4,512]{0,2,1:T(8,128)(2,1)S(1)}, u32[]{:S(2)}, u32[]{:S(2)}) async-start(bf16[256,4,512]{0,2,1:T(8,128)(2,1)} %bitcast.35), calls=%async_computation.2 | async-start | bytes 2097152 | tf_op jit(solution)/shard_map/all_to_all | solution.py:64
  225.4 19.1 %copy-start.1 = (bf16[256,4,512]{2,0,1:T(8,128)(2,1)S(1)}, bf16[256,4,512]{2,0,1:T(8,128)(2,1)}, u32[]{:S(2)}) copy-start(bf16[256,4,512]{2,0,1:T(8,128)(2,1)} %copy-done) | copy-start | bytes 3145732
  240.2 31.3 %all-to-all-start.6 = ((bf16[256,4,512]{0,2,1:T(8,128)(2,1)}), bf16[256,4,512]{0,2,1:T(8,128)(2,1)}, u32[]{:S(2)}, u32[]{:S(2)}) async-start(bf16[256,4,512]{0,2,1:T(8,128)(2,1)} %bitcast.83), calls=%async_computation.6 | async-start | bytes 2097152 | tf_op jit(solution)/shard_map/all_to_all | solution.py:64
  245.8 1.3 copy-start.3
  271.5 29.6 %all-to-all-start.3 = ((bf16[4,256,512]{2,1,0:T(8,128)(2,1)}), bf16[4,256,512]{2,1,0:T(8,128)(2,1)S(1)}, u32[]{:S(2)}, u32[]{:S(2)}) async-start(bf16[4,256,512]{2,1,0:T(8,128)(2,1)} %bitcast.39), calls=%async_computation.3 | async-start | bytes 2097152 | tf_op jit(solution)/shard_map/all_to_all | solution.py:70
  301.2 28.8 %all-to-all-start.7 = ((bf16[4,256,512]{2,1,0:T(8,128)(2,1)}), bf16[4,256,512]{2,1,0:T(8,128)(2,1)S(1)}, u32[]{:S(2)}, u32[]{:S(2)}) async-start(bf16[4,256,512]{2,1,0:T(8,128)(2,1)} %bitcast.54), calls=%async_computation.7 | async-start | bytes 2097152 | tf_op jit(solution)/shard_map/all_to_all | solution.py:70
Sparse Core Ops, SparseCore 0:
  9.5 76.9 all-gather.2
  88.1 72.5 all-gather.4
where the time goes:
time: 340 us; the launch traced here: 339 us
  waiting for transfers between devices  230 us (68%)
  starting transfers between devices  37.6 us (11%)
  other arithmetic  24 us (7%)
  local copies, waits for them, and re-layouts  19.9 us (6%)
  between operations  14.3 us (4%)
  matrix products  12.7 us (4%)
    all_to_all x4, waiting for transfers between devices, to_cells(): lax.all_to_all(field.reshape(field.shape[0], -1), 'chan', split_axis=1, c...  91.9 us
    all_to_all x4, waiting for transfers between devices, to_channels(): lax.all_to_all(field, 'chan', split_axis=0, concat_axis=1, tiled=True)  63.2 us
    all_gather x1, waiting for transfers between devices, body(): lax.all_gather(weight_out, 'chan', axis=0, tiled=True)  58.4 us
    all_to_all x4, starting transfers between devices, to_cells(): lax.all_to_all(field.reshape(field.shape[0], -1), 'chan', split_axis=1, c...  17.6 us
    all_gather x1, waiting for transfers between devices, body(): lax.all_gather(weight_in, 'chan', axis=0, tiled=True)  15.1 us
    all_to_all x4, starting transfers between devices, to_channels(): lax.all_to_all(field, 'chan', split_axis=0, concat_axis=1, tiled=True)  14.4 us
    convert_element_type x1, other arithmetic, body(): core(padded_grad, filter_taps, -1).astype(jnp.bfloat16).reshape(slab_shape)  10 us
    convert_element_type x1, other arithmetic, body(): mix_grad = (act_grad.astype(jnp.float32).reshape(slope.shape) * slope).as...  10 us
  transfers between devices with their start and end apart: 14, of which 9 were waited for; matrix products, arithmetic and copies ran while one was open for 13% of the time, Pallas kernels for 0%

commit v1 on v0

--- a/solution.py
+++ b/solution.py
@@ -61,8 +61,14 @@
 
 
 def to_cells(field):
-    return lax.all_to_all(
-        field.reshape(field.shape[0], -1), "chan", split_axis=1, concat_axis=0, tiled=True
+    return jnp.concatenate(
+        lax.all_to_all(
+            jnp.stack(jnp.split(field.reshape(field.shape[0], -1), lax.axis_size("chan"), 1), 0),
+            "chan",
+            0,
+            0,
+        ),
+        0,
     )
 
 

time: 340 us -> 340 us (level)
    another operation x0 -> x4, other arithmetic: none -> 4.45 us  [to_cells(): jnp.stack(jnp.split(field.reshape(field.shape[0], -1), lax.axis_size('cha...]
where the time goes in v1:
time: 340 us; the launch traced here: 339 us
  waiting for transfers between devices  229 us (67%)
  starting transfers between devices  37.5 us (11%)
  other arithmetic  26.8 us (8%)
  local copies, waits for them, and re-layouts  17.8 us (5%)
  between operations  14.4 us (4%)
  matrix products  12.8 us (4%)
    all_to_all x4, waiting for transfers between devices, to_cells(): lax.all_to_all(jnp.stack(jnp.split(field.reshape(field.shape[0], -1), lax...  91.1 us
    all_to_all x4, waiting for transfers between devices, to_channels(): lax.all_to_all(field, 'chan', split_axis=0, concat_axis=1, tiled=True)  63.4 us
    all_gather x1, waiting for transfers between devices, body(): lax.all_gather(weight_out, 'chan', axis=0, tiled=True)  58.3 us
    all_to_all x4, starting transfers between devices, to_cells(): lax.all_to_all(jnp.stack(jnp.split(field.reshape(field.shape[0], -1), lax...  17.8 us
    all_gather x1, waiting for transfers between devices, body(): lax.all_gather(weight_in, 'chan', axis=0, tiled=True)  15.2 us
    all_to_all x4, starting transfers between devices, to_channels(): lax.all_to_all(field, 'chan', split_axis=0, concat_axis=1, tiled=True)  14.2 us
    convert_element_type x1, other arithmetic, body(): mix_grad = (act_grad.astype(jnp.float32).reshape(slope.shape) * slope).as...  10 us
    convert_element_type x1, other arithmetic, body(): core(padded_grad, filter_taps, -1).astype(jnp.bfloat16).reshape(slab_shape)  9.32 us
  transfers between devices with their start and end apart: 14, of which 9 were waited for; matrix products, arithmetic and copies ran while one was open for 13% of the time, Pallas kernels for 0%

profile of v1, /device:TPU:0, one launch (start us, length us, event | category | flops | bytes accessed | tf_op | source)
XLA Modules:
  0.0 338.7 jit_solution(14345214376379707854)
XLA Ops:
  10.6 6.3 %all-to-all-start = ((bf16[4,256,512]{2,1,0:T(8,128)(2,1)}), bf16[4,256,512]{2,1,0:T(8,128)(2,1)S(1)}, u32[]{:S(2)}, u32[]{:S(2)}) async-start(bf16[4,256,512]{2,1,0:T(8,128)(2,1)} %pad_maximum_fusion), calls=%async_computation | async-start | bytes 2097152 | tf_op jit(solution)/shard_map/all_to_all | solution.py:65
  19.2 48.9 %all-to-all-done = bf16[4,256,512]{2,1,0:T(8,128)(2,1)S(1)} async-done(((bf16[4,256,512]{2,1,0:T(8,128)(2,1)}), bf16[4,256,512]{2,1,0:T(8,128)(2,1)S(1)}, u32[]{:S(2)}, u32[]{:S(2)}) %all-to-all-start) | async-done | bytes 1048608 | tf_op jit(solution)/shard_map/all_to_all | solution.py:65
  68.1 3.5 %all-to-all-start.4 = ((bf16[4,256,512]{2,1,0:T(8,128)(2,1)}), bf16[4,256,512]{2,1,0:T(8,128)(2,1)S(1)}, u32[]{:S(2)}, u32[]{:S(2)}) async-start(bf16[4,256,512]{2,1,0:T(8,128)(2,1)} %pad_maximum_fusion.2), calls=%async_computation.4 | async-start | bytes 2097152 | tf_op jit(solution)/shard_map/all_to_all | solution.py:65
  71.6 15.2 %all-gather.3.cloned.1.call-done = bf16[1024,1024]{1,0:T(8,128)(2,1)} async-done(((bf16[256,1024]{1,0:T(8,128)(2,1)}), bf16[1024,1024]{1,0:T(8,128)(2,1)}) %all-gather.3.cloned.1.call-update) | async-done | bytes 2097168 | tf_op jit(solution)/shard_map/all_gather | solution.py:85
  86.9 2.9 convolution_convert_fusion.1
  90.8 8.1 %all-to-all-done.4 = bf16[4,256,512]{2,1,0:T(8,128)(2,1)S(1)} async-done(((bf16[4,256,512]{2,1,0:T(8,128)(2,1)}), bf16[4,256,512]{2,1,0:T(8,128)(2,1)S(1)}, u32[]{:S(2)}, u32[]{:S(2)}) %all-to-all-start.4) | async-done | bytes 1048608 | tf_op jit(solution)/shard_map/all_to_all | solution.py:65
  99.0 3.5 %all-to-all-start.1 = ((bf16[4,256,512]{1,2,0:T(8,128)(2,1)}), bf16[4,256,512]{1,2,0:T(8,128)(2,1)S(1)}, u32[]{:S(2)}, u32[]{:S(2)}) async-start(bf16[4,256,512]{1,2,0:T(8,128)(2,1)} %bitcast.109), calls=%async_computation.1 | async-start | bytes 2097152 | tf_op jit(solution)/shard_map/all_to_all | solution.py:76
  102.5 58.3 %all-gather.5.cloned.1.call-done = bf16[1024,1024]{1,0:T(8,128)(2,1)} async-done(((bf16[256,1024]{1,0:T(8,128)(2,1)}), bf16[1024,1024]{1,0:T(8,128)(2,1)}) %all-gather.5.cloned.1.call-update) | async-done | bytes 2097168 | tf_op jit(solution)/shard_map/all_gather | solution.py:86
  160.8 2.9 convolution_convert_fusion
  164.7 3.6 %all-to-all-start.5 = ((bf16[4,256,512]{1,2,0:T(8,128)(2,1)}), bf16[4,256,512]{1,2,0:T(8,128)(2,1)S(1)}, u32[]{:S(2)}, u32[]{:S(2)}) async-start(bf16[4,256,512]{1,2,0:T(8,128)(2,1)} %bitcast.119), calls=%async_computation.5 | async-start | bytes 2097152 | tf_op jit(solution)/shard_map/all_to_all | solution.py:76
  172.1 22.0 %all-to-all-done.5 = bf16[4,256,512]{1,2,0:T(8,128)(2,1)S(1)} async-done(((bf16[4,256,512]{1,2,0:T(8,128)(2,1)}), bf16[4,256,512]{1,2,0:T(8,128)(2,1)S(1)}, u32[]{:S(2)}, u32[]{:S(2)}) %all-to-all-start.5) | async-done | bytes 1048608 | tf_op jit(solution)/shard_map/all_to_all | solution.py:76
  195.6 10.0 %fusion.5 = (bf16[256,4,16,32]{0,3,2,1:T(8,128)(2,1)S(1)}, f32[256,4,16,32]{0,3,2,1:T(8,128)S(1)}) fusion(f32[256,4,16,32]{0,3,2,1:T(8,128)S(1)} %bitcast.112, f32[256]{0:T(256)S(1)} %copy-done.5, f32[256]{0:T(256)S(1)} %bitcast.145, f32[256]{0:T(256)S(1)} %bitcast.147, f32[256]{0:T(256)S(1)} %bitcast.151, f32[256]{0:T(256)S(1)} %bitcast.153, ...), kind=kLoop, calls=%fused_computation.54 | loop fusion | flops 33554432 | bytes 14708736 | tf_op jit(solution)/shard_map/convert_element_type | solution.py:109
  210.7 3.5 %all-to-all-start.2 = ((bf16[4,256,512]{1,2,0:T(8,128)(2,1)}), bf16[4,256,512]{1,2,0:T(8,128)(2,1)S(1)}, u32[]{:S(2)}, u32[]{:S(2)}) async-start(bf16[4,256,512]{1,2,0:T(8,128)(2,1)} %pad_maximum_fusion.1), calls=%async_computation.2 | async-start | bytes 2097152 | tf_op jit(solution)/shard_map/all_to_all | solution.py:65
  215.4 9.3 %fusion.104 = bf16[256,4,16,32]{0,3,2,1:T(8,128)(2,1)S(1)} fusion(f32[256,6,16,32]{0,3,2,1:T(8,128)S(1)} %maximum_convert_fusion.1, f32[256]{0:T(256)S(1)} %bitcast.146, f32[256]{0:T(256)S(1)} %bitcast.148, f32[256]{0:T(256)S(1)} %bitcast.152, f32[256]{0:T(256)S(1)} %bitcast.154, f32[256]{0:T(256)S(1)} %bitcast.156, f32[256]{0:T(256)S(1)} %bitcast.158, ...), kind=kLoop, calls=%fused_computation.153 | loop fusion | flops 28311552 | bytes 10513408 | tf_op jit(solution)/shard_map/convert_element_type | solution.py:113
  226.0 14.3 %all-to-all-done.2 = bf16[4,256,512]{1,2,0:T(8,128)(2,1)S(1)} async-done(((bf16[4,256,512]{1,2,0:T(8,128)(2,1)}), bf16[4,256,512]{1,2,0:T(8,128)(2,1)S(1)}, u32[]{:S(2)}, u32[]{:S(2)}) %all-to-all-start.2) | async-done | bytes 1048608 | tf_op jit(solution)/shard_map/all_to_all | solution.py:65
  240.3 4.4 %all-to-all-start.6 = ((bf16[4,256,512]{1,2,0:T(8,128)(2,1)}), bf16[4,256,512]{1,2,0:T(8,128)(2,1)}, u32[]{:S(2)}, u32[]{:S(2)}) async-start(bf16[4,256,512]{1,2,0:T(8,128)(2,1)} %pad_maximum_fusion.3), calls=%async_computation.6 | async-start | bytes 2097152 | tf_op jit(solution)/shard_map/all_to_all | solution.py:65
  247.4 3.2 fusion.109
  251.9 19.7 %all-to-all-done.6 = bf16[4,256,512]{1,2,0:T(8,128)(2,1)} async-done(((bf16[4,256,512]{1,2,0:T(8,128)(2,1)}), bf16[4,256,512]{1,2,0:T(8,128)(2,1)}, u32[]{:S(2)}, u32[]{:S(2)}) %all-to-all-start.6) | async-done | bytes 1048608 | tf_op jit(solution)/shard_map/all_to_all | solution.py:65
  271.6 3.5 %all-to-all-start.3 = ((bf16[4,256,512]{2,1,0:T(8,128)(2,1)}), bf16[4,256,512]{2,1,0:T(8,128)(2,1)S(1)}, u32[]{:S(2)}, u32[]{:S(2)}) async-start(bf16[4,256,512]{2,1,0:T(8,128)(2,1)} %bitcast.44), calls=%async_computation.3 | async-start | bytes 2097152 | tf_op jit(solution)/shard_map/all_to_all | solution.py:76
  277.2 3.8 %fusion.108 = bf16[1024,512]{0,1:T(8,128)(2,1)} fusion(bf16[1024,512]{0,1:T(8,128)(2,1)S(1)} %copy.48, bf16[1024,512]{1,0:T(8,128)(2,1)S(1)} %bitcast.129, bf16[1024,1024]{1,0:T(8,128)(2,1)} %all-gather.3.cloned.1.call-done), kind=kOutput, calls=%fused_computation.164 | convolution fusion | flops 1075314688 | bytes 5242880 | tf_op jit(solution)/shard_map/dot_general | solution.py:115
  281.0 2.3 copy.49
  283.3 17.9 %all-to-all-done.3 = bf16[4,256,512]{2,1,0:T(8,128)(2,1)S(1)} async-done(((bf16[4,256,512]{2,1,0:T(8,128)(2,1)}), bf16[4,256,512]{2,1,0:T(8,128)(2,1)S(1)}, u32[]{:S(2)}, u32[]{:S(2)}) %all-to-all-start.3) | async-done | bytes 1048608 | tf_op jit(solution)/shard_map/all_to_all | solution.py:76
  301.3 3.5 %all-to-all-start.7 = ((bf16[4,256,512]{2,1,0:T(8,128)(2,1)}), bf16[4,256,512]{2,1,0:T(8,128)(2,1)S(1)}, u32[]{:S(2)}, u32[]{:S(2)}) async-start(bf16[4,256,512]{2,1,0:T(8,128)(2,1)} %bitcast.64), calls=%async_computation.7 | async-start | bytes 2097152 | tf_op jit(solution)/shard_map/all_to_all | solution.py:76
  306.6 23.5 %all-to-all-done.7 = bf16[4,256,512]{2,1,0:T(8,128)(2,1)S(1)} async-done(((bf16[4,256,512]{2,1,0:T(8,128)(2,1)}), bf16[4,256,512]{2,1,0:T(8,128)(2,1)S(1)}, u32[]{:S(2)}, u32[]{:S(2)}) %all-to-all-start.7) | async-done | bytes 1048608 | tf_op jit(solution)/shard_map/all_to_all | solution.py:76
  (52 shorter events, 29.8 us)
Async XLA Ops:
  7.2 79.7 %all-gather.3.cloned.1.call-start = ((), (), s32[]{:S(2)}) async-start(), calls=%async_computation.8 | async-start | bytes 2621440 | tf_op jit(solution)/shard_map/all_gather | solution.py:85
  9.5 8.2 %copy-start.2 = (bf16[256,4,512]{2,1,0:T(4,128)(2,1)S(1)}, bf16[256,4,512]{2,1,0:T(4,128)(2,1)}, u32[]{:S(2)}) copy-start(bf16[256,4,512]{2,1,0:T(4,128)(2,1)} %param.7) | copy-start | bytes 3145732
  10.6 57.5 %all-to-all-start = ((bf16[4,256,512]{2,1,0:T(8,128)(2,1)}), bf16[4,256,512]{2,1,0:T(8,128)(2,1)S(1)}, u32[]{:S(2)}, u32[]{:S(2)}) async-start(bf16[4,256,512]{2,1,0:T(8,128)(2,1)} %pad_maximum_fusion), calls=%async_computation | async-start | bytes 2097152 | tf_op jit(solution)/shard_map/all_to_all | solution.py:65
  17.0 143.8 %all-gather.5.cloned.1.call-start = ((), (), s32[]{:S(2)}) async-start(), calls=%async_computation.9 | async-start | bytes 2621440 | tf_op jit(solution)/shard_map/all_gather | solution.py:86
  68.1 21.7 %copy-start = (bf16[4,256,512]{2,1,0:T(8,128)(2,1)}, bf16[4,256,512]{2,1,0:T(8,128)(2,1)S(1)}, u32[]{:S(2)}) copy-start(bf16[4,256,512]{2,1,0:T(8,128)(2,1)S(1)} %all-to-all-done) | copy-start | bytes 3145732
  68.1 30.9 %all-to-all-start.4 = ((bf16[4,256,512]{2,1,0:T(8,128)(2,1)}), bf16[4,256,512]{2,1,0:T(8,128)(2,1)S(1)}, u32[]{:S(2)}, u32[]{:S(2)}) async-start(bf16[4,256,512]{2,1,0:T(8,128)(2,1)} %pad_maximum_fusion.2), calls=%async_computation.4 | async-start | bytes 2097152 | tf_op jit(solution)/shard_map/all_to_all | solution.py:65
  99.0 65.7 %all-to-all-start.1 = ((bf16[4,256,512]{1,2,0:T(8,128)(2,1)}), bf16[4,256,512]{1,2,0:T(8,128)(2,1)S(1)}, u32[]{:S(2)}, u32[]{:S(2)}) async-start(bf16[4,256,512]{1,2,0:T(8,128)(2,1)} %bitcast.109), calls=%async_computation.1 | async-start | bytes 2097152 | tf_op jit(solution)/shard_map/all_to_all | solution.py:76
  164.7 7.4 %copy-start.4 = (f32[256,27]{0,1:T(8,128)S(1)}, f32[256,27]{0,1:T(8,128)}, u32[]{:S(2)}) copy-start(f32[256,27]{0,1:T(8,128)} %param.10) | copy-start | bytes 82948
  164.7 29.5 %all-to-all-start.5 = ((bf16[4,256,512]{1,2,0:T(8,128)(2,1)}), bf16[4,256,512]{1,2,0:T(8,128)(2,1)S(1)}, u32[]{:S(2)}, u32[]{:S(2)}) async-start(bf16[4,256,512]{1,2,0:T(8,128)(2,1)} %bitcast.119), calls=%async_computation.5 | async-start | bytes 2097152 | tf_op jit(solution)/shard_map/all_to_all | solution.py:76
  169.2 25.2 %collective-permute-start = (bf16[256,1,512]{0,2,1:T(8,128)(2,1)}, bf16[256,1,512]{0,2,1:T(8,128)(2,1)S(1)}, u32[]{:S(2)}, u32[]{:S(2)}) collective-permute-start(bf16[256,1,512]{0,2,1:T(8,128)(2,1)} %get-tuple-element.16), channel_id=1, source_target_pairs={{0,1},{1,2},{2,3},{4,5},{5,6},{6,7},{8,9},{9,10},{10,11},{12,13},{... | collective-permute-start | bytes 786440 | tf_op jit(solution)/shard_map/ppermute | solution.py:17
  170.8 23.6 %collective-permute-start.1 = (bf16[256,1,512]{0,2,1:T(8,128)(2,1)}, bf16[256,1,512]{0,2,1:T(8,128)(2,1)}, u32[]{:S(2)}, u32[]{:S(2)}) collective-permute-start(bf16[256,1,512]{0,2,1:T(8,128)(2,1)} %get-tuple-element.17), channel_id=1, source_target_pairs={{1,0},{2,1},{3,2},{5,4},{6,5},{7,6},{9,8},{10,9},{11,10},{13,12},{... | collective-permute-start | bytes 786440 | tf_op jit(solution)/shard_map/ppermute | solution.py:20
  194.4 1.2 copy-start.5
  206.9 7.3 %collective-permute-start.2 = (bf16[256,1,512]{0,2,1:T(8,128)(2,1)}, bf16[256,1,512]{0,2,1:T(8,128)(2,1)S(1)}, u32[]{:S(2)}, u32[]{:S(2)}) collective-permute-start(bf16[256,1,512]{0,2,1:T(8,128)(2,1)} %get-tuple-element.10), channel_id=1, source_target_pairs={{0,1},{1,2},{2,3},{4,5},{5,6},{6,7},{8,9},{9,10},{10,11},{12,13},{... | collective-permute-start | bytes 786440 | tf_op jit(solution)/shard_map/ppermute | solution.py:17
  208.2 6.0 %collective-permute-start.3 = (bf16[256,1,512]{0,2,1:T(8,128)(2,1)}, bf16[256,1,512]{0,2,1:T(8,128)(2,1)}, u32[]{:S(2)}, u32[]{:S(2)}) collective-permute-start(bf16[256,1,512]{0,2,1:T(8,128)(2,1)} %get-tuple-element.11), channel_id=1, source_target_pairs={{1,0},{2,1},{3,2},{5,4},{6,5},{7,6},{9,8},{10,9},{11,10},{13,12},{... | collective-permute-start | bytes 786440 | tf_op jit(solution)/shard_map/ppermute | solution.py:20
  210.7 29.6 %all-to-all-start.2 = ((bf16[4,256,512]{1,2,0:T(8,128)(2,1)}), bf16[4,256,512]{1,2,0:T(8,128)(2,1)S(1)}, u32[]{:S(2)}, u32[]{:S(2)}) async-start(bf16[4,256,512]{1,2,0:T(8,128)(2,1)} %pad_maximum_fusion.1), calls=%async_computation.2 | async-start | bytes 2097152 | tf_op jit(solution)/shard_map/all_to_all | solution.py:65
  224.8 19.9 %copy-start.1 = (bf16[4,256,512]{2,1,0:T(8,128)(2,1)S(1)}, bf16[4,256,512]{2,1,0:T(8,128)(2,1)}, u32[]{:S(2)}) copy-start(bf16[4,256,512]{2,1,0:T(8,128)(2,1)} %copy-done) | copy-start | bytes 3145732
  240.3 31.3 %all-to-all-start.6 = ((bf16[4,256,512]{1,2,0:T(8,128)(2,1)}), bf16[4,256,512]{1,2,0:T(8,128)(2,1)}, u32[]{:S(2)}, u32[]{:S(2)}) async-start(bf16[4,256,512]{1,2,0:T(8,128)(2,1)} %pad_maximum_fusion.3), calls=%async_computation.6 | async-start | bytes 2097152 | tf_op jit(solution)/shard_map/all_to_all | solution.py:65
  246.1 1.3 copy-start.3
  271.6 29.6 %all-to-all-start.3 = ((bf16[4,256,512]{2,1,0:T(8,128)(2,1)}), bf16[4,256,512]{2,1,0:T(8,128)(2,1)S(1)}, u32[]{:S(2)}, u32[]{:S(2)}) async-start(bf16[4,256,512]{2,1,0:T(8,128)(2,1)} %bitcast.44), calls=%async_computation.3 | async-start | bytes 2097152 | tf_op jit(solution)/shard_map/all_to_all | solution.py:76
  301.3 28.8 %all-to-all-start.7 = ((bf16[4,256,512]{2,1,0:T(8,128)(2,1)}), bf16[4,256,512]{2,1,0:T(8,128)(2,1)S(1)}, u32[]{:S(2)}, u32[]{:S(2)}) async-start(bf16[4,256,512]{2,1,0:T(8,128)(2,1)} %bitcast.64), calls=%async_computation.7 | async-start | bytes 2097152 | tf_op jit(solution)/shard_map/all_to_all | solution.py:76
Sparse Core Ops, SparseCore 0:
  9.5 77.2 all-gather.2
  88.4 72.3 all-gather.4
